TPU v7x, 128 devices: a whole 4x4x4 slice. The times are simulated.
128 devices in a mesh: brick: 64 (over z_lo, x, y, core), vec: 2 (over z_hi).
Axes of the slice: x: 4, y: 4, z: 4 (z_hi: 2, z_lo: 2; z = z_hi * 2 + z_lo), core: 2. Of those that a mesh axis runs over, the one named last changes fastest.
Arguments:
- levels: int32 [12, 2048, 16, 128], P(None, 'brick'), may hold values from 0 to 255
- start_block: int32 [16, 2048, 16, 128], P('vec', 'brick'), may hold values from -8 to 8
Outputs:
- alpha_blocks: float32 [1, 16, 16], replicated
- beta_blocks: float32 [1, 16, 16], replicated
- basis: float32 [16, 2048, 16, 128], P('vec', 'brick')
All inputs are finite; a program needn't handle non-finite values.
Results may differ from a plain program's by a relative error of at most 0.00026.
Values sent between devices are 32-bit elements; how exact they have to be, the bound alone decides.
No kernel may reach another device: no remote copies, remote signals or barrier semaphores. Data moves between devices by JAX's collectives and lax.ppermute only.
A program may use at most 128 MiB of HBM per device.

v0:
```python
import math
import jax
import jax.numpy as jnp
from jax import lax
from jax.sharding import PartitionSpec as P

offsets_cube = (1, 3, 9, 27)
deepest = 27
highest = lax.Precision.HIGHEST


def passed_along(value, axis, by):
    size = lax.axis_size(axis)
    pairs = [(i, i + by) for i in range(size) if 0 <= i + by < size]
    return lax.ppermute(value, axis, pairs)


def forward_take(field_in, offset, axis_dim):
    length_dim = field_in.shape[axis_dim]
    widths = [(0, 0)] * field_in.ndim
    widths[axis_dim] = (0, offset)
    return lax.slice_in_dim(jnp.pad(field_in, widths), offset, offset + length_dim, axis=axis_dim)


def backward_put(field_in, offset, axis_dim):
    length_dim = field_in.shape[axis_dim]
    widths = [(0, 0)] * field_in.ndim
    widths[axis_dim] = (offset, 0)
    return lax.slice_in_dim(jnp.pad(field_in, widths), 0, length_dim, axis=axis_dim)


def local_planes(field_in, weights, result):
    for axis_dim in (2, 3):
        for position, offset in enumerate(offsets_cube):
            channel = weights[4 * (axis_dim - 1) + position]
            result = (
                result
                + channel * forward_take(field_in, offset, axis_dim)
                + backward_put(channel * field_in, offset, axis_dim)
            )
    return result


def apply_carried(field_in, weights):
    row_count = field_in.shape[1]
    upper_rows = passed_along(field_in[:, :deepest], "brick", -1)
    extended = jnp.concatenate([field_in, upper_rows], axis=1)
    result = jnp.zeros_like(field_in)
    spilled = jnp.zeros_like(upper_rows)
    for position, offset in enumerate(offsets_cube):
        channel = weights[position]
        result = result + channel * extended[:, offset : offset + row_count]
        shifted_rows = jnp.pad(
            channel * field_in, ((0, 0), (offset, deepest - offset), (0, 0), (0, 0))
        )
        result = result + shifted_rows[:, :row_count]
        spilled = spilled + shifted_rows[:, row_count:]
    result = local_planes(field_in, weights, result)
    arrived = passed_along(spilled, "brick", 1)
    return result + jnp.pad(arrived, ((0, 0), (0, row_count - deepest), (0, 0), (0, 0)))


def inner_of(left_rows, right_rows):
    return jnp.einsum("in,jn->ij", left_rows, right_rows, precision=highest)


def body(levels, start_block):
    weights = (levels.astype(jnp.float32) + 0.5) / 256.0

    def affinity_apply(field_in):
        return apply_carried(field_in, weights)

    unit_field = jnp.ones((1,) + levels.shape[1:], jnp.float32)
    degree = affinity_apply(unit_field)[0] + 1.0
    inv_root = lax.rsqrt(degree)

    def half_step(block_in):
        return 0.5 * (block_in + inv_root * affinity_apply(inv_root * block_in))

    own_cols = start_block.shape[0]
    grid_shape = start_block.shape
    voxel_total = lax.axis_size("brick") * grid_shape[1] * grid_shape[2] * grid_shape[3]

    def to_work(block_in):
        flat_block = block_in.reshape(own_cols, -1)
        work_rows = lax.all_gather(flat_block, "vec", axis=0, tiled=True)
        return work_rows

    def from_work(work_rows):
        own_rows = lax.dynamic_slice_in_dim(
            work_rows, lax.axis_index("vec") * own_cols, own_cols, 0
        )
        return own_rows.reshape(grid_shape)

    def total_one(partial_sum):
        summed = lax.psum(partial_sum, "brick")
        return summed

    start_work = to_work(start_block.astype(jnp.float32))
    lower_factor = jnp.linalg.cholesky(total_one(inner_of(start_work, start_work)))
    current = lax.linalg.triangular_solve(lower_factor, start_work, left_side=True, lower=True)
    basis_now = from_work(current)
    image_block = to_work(half_step(half_step(basis_now)))
    coeffs = total_one(inner_of(image_block, current))
    residual = image_block - jnp.einsum("ij,jn->in", coeffs, current, precision=highest)
    gram_matrix = total_one(inner_of(residual, residual))
    lower_factor = jnp.linalg.cholesky(gram_matrix)
    following = lax.linalg.triangular_solve(lower_factor, residual, left_side=True, lower=True)
    alpha_list = [coeffs]
    beta_list = [lower_factor]
    basis_now = from_work(following)
    basis = basis_now * math.sqrt(voxel_total)
    return (jnp.stack(alpha_list), jnp.stack(beta_list), basis)


def solution(mesh):
    return jax.shard_map(
        body,
        mesh=mesh,
        in_specs=(P(None, "brick", None, None), P("vec", "brick", None, None)),
        out_specs=(P(), P(), P("vec", "brick", None, None)),
        check_vma=False,
    )
```

profile of v0, /device:TPU:1, one launch (start us, length us, event | category | flops | bytes accessed | tf_op | source)
XLA Modules:
  0.0 726.9 jit_solution(13446341821634345445)
XLA Ops:
  9.0 2.5 copy.14
  12.3 3.3 collective-permute-start
  20.1 3.2 collective-permute-start.1
  26.5 2.7 broadcast_multiply_fusion.24
  29.2 48.8 %all-gather.3.cloned.1.call-done = f32[16,65536]{1,0:T(8,128)} async-done(((f32[8,65536]{1,0:T(8,128)}), f32[16,65536]{1,0:T(8,128)}) %all-gather.3.cloned.1.call-update) | async-done | bytes 4194320 | tf_op jit(solution)/shard_map/all_gather | solution.py:86
  78.0 9.0 %fusion.127 = f32[16,16]{0,1:T(8,128)S(1)} fusion(f32[16,65536]{1,0:T(8,128)} %all-gather.3.cloned.1.call-done), kind=kOutput, calls=%fused_computation.264 | convolution fusion | flops 201326592 | bytes 4195328 | tf_op jit(solution)/shard_map/in,jn->ij/dot_general | solution.py:64
  87.0 140.6 %psum.21 = f32[16,16]{0,1:T(8,128)S(1)} all-reduce(f32[16,16]{0,1:T(8,128)S(1)} %fusion.127), channel_id=1, replica_groups=mesh['brick'=64,'vec'=2] {'brick'}, use_global_device_ids=true, to_apply=%region_0.1 | all-reduce | flops 256 | bytes 2048 | tf_op jit(solution)/shard_map/psum | solution.py:96
  231.7 5.4 fusion.122
  241.4 4.7 collective-permute-start.2
  246.1 5.1 broadcast_multiply_fusion.12
  254.7 10.7 %collective-permute-done.2 = f32[8,27,16,128]{3,0,2,1:T(8,128)S(1)} collective-permute-done((f32[8,27,16,128]{3,0,2,1:T(8,128)S(1)}, f32[8,27,16,128]{3,0,2,1:T(8,128)S(1)}, u32[]{:S(2)}, u32[]{:S(2)}) %collective-permute-start.2) | collective-permute-done | bytes 1769504 | tf_op jit(solution)/shard_map/ppermute | solution.py:15
  265.3 8.6 %collective-permute-done.3 = f32[8,27,16,128]{3,0,2,1:T(8,128)S(1)} collective-permute-done((f32[8,27,16,128]{3,0,2,1:T(8,128)S(1)}, f32[8,27,16,128]{3,0,2,1:T(8,128)S(1)}, u32[]{:S(2)}, u32[]{:S(2)}) %collective-permute-start.3) | collective-permute-done | bytes 1769504 | tf_op jit(solution)/shard_map/ppermute | solution.py:15
  275.2 12.9 %broadcast_multiply_fusion.13 = (f32[8,32,16,128]{3,0,2,1:T(8,128)}, f32[8,32,16,128]{3,0,2,1:T(8,128)S(1)}, f32[8,32,16,128]{3,0,2,1:T(8,128)}) fusion(f32[32,16,128]{2,1,0:T(8,128)} %get-tuple-element.20, f32[32,16,128]{2,1,0:T(8,128)} %get-tuple-element.11, f32[8,32,16,128]{3,0,2,1:T(8,128)} %bitcast.67, f32[8,27,16,128]{3,0,2,1:T(8,128)} %copy-done.32, ...), kind=kLoop, calls=%fused_computation.155 | loop fusion | flops 22020096 | bytes 40763392 | tf_op jit(solution)/shard_map/mul | solution.py:39
  289.6 5.1 broadcast_multiply_fusion.11
  296.8 4.5 collective-permute-start.5
  301.3 17.9 %collective-permute-done.4 = f32[8,27,16,128]{3,0,2,1:T(8,128)S(1)} collective-permute-done((f32[8,27,16,128]{3,0,2,1:T(8,128)S(1)}, f32[8,27,16,128]{3,0,2,1:T(8,128)S(1)}, u32[]{:S(2)}, u32[]{:S(2)}) %collective-permute-start.4) | collective-permute-done | bytes 1769504 | tf_op jit(solution)/shard_map/ppermute | solution.py:15
  322.0 11.3 %add_multiply_fusion.1 = f32[8,32,16,128]{3,0,2,1:T(8,128)} fusion(f32[8,32,16,128]{3,0,2,1:T(8,128)} %get-tuple-element.10, f32[8,27,16,128]{3,0,2,1:T(8,128)} %copy-done.30, f32[8,32,16,128]{3,0,2,1:T(8,128)} %get-tuple-element.40, f32[8,32,16,128]{3,0,2,1:T(8,128)S(1)} %get-tuple-element.9, f32[8,32,16,128]{3,0,2,1:T(8,128)} %get-tuple-element.47, ...), kind=kLoop, calls=%fused_computation.134 | loop fusion | flops 22020096 | bytes 36306944 | tf_op jit(solution)/shard_map/mul | solution.py:78
  333.3 65.7 %all-gather.5.cloned.1.call-done = f32[16,65536]{1,0:T(8,128)} async-done(((f32[8,65536]{1,0:T(8,128)}), f32[16,65536]{1,0:T(8,128)}) %all-gather.5.cloned.1.call-update) | async-done | bytes 4194320 | tf_op jit(solution)/shard_map/all_gather | solution.py:86
  399.0 8.7 %fusion.128 = f32[16,16]{1,0:T(8,128)S(1)} fusion(f32[16,65536]{1,0:T(8,128)} %all-gather.5.cloned.1.call-done, f32[16,65536]{1,0:T(8,128)} %copy-done.1), kind=kOutput, calls=%fused_computation.265 | convolution fusion | flops 201326592 | bytes 8389632 | tf_op jit(solution)/shard_map/in,jn->ij/dot_general | solution.py:64
  407.7 140.9 %psum.22 = f32[16,16]{1,0:T(8,128)S(1)} all-reduce(f32[16,16]{1,0:T(8,128)S(1)} %fusion.128), channel_id=1, replica_groups=mesh['brick'=64,'vec'=2] {'brick'}, use_global_device_ids=true, to_apply=%region_3.6 | all-reduce | flops 256 | bytes 2048 | tf_op jit(solution)/shard_map/psum | solution.py:96
  548.6 7.1 convolution_subtract_fusion
  557.7 5.6 fusion.129
  563.3 144.8 %psum.23 = f32[16,16]{0,1:T(8,128)S(1)} all-reduce(f32[16,16]{0,1:T(8,128)S(1)} %fusion.129), channel_id=1, replica_groups=mesh['brick'=64,'vec'=2] {'brick'}, use_global_device_ids=true, to_apply=%region_4.7 | all-reduce | flops 256 | bytes 2048 | tf_op jit(solution)/shard_map/psum | solution.py:96
  712.8 5.4 fusion.119
  (108 shorter events, 37.8 us)
Async XLA Ops:
  7.2 70.8 %all-gather.3.cloned.1.call-start = ((), (), s32[]{:S(2)}) async-start(), calls=%async_computation | async-start | bytes 6291456 | tf_op jit(solution)/shard_map/all_gather | solution.py:86
  11.5 387.5 %all-gather.5.cloned.1.call-start = ((), (), s32[]{:S(2)}) async-start(), calls=%async_computation.1 | async-start | bytes 6291456 | tf_op jit(solution)/shard_map/all_gather | solution.py:86
  12.3 12.7 %collective-permute-start = (f32[1,27,16,128]{3,2,1,0:T(8,128)}, f32[1,27,16,128]{3,2,1,0:T(8,128)}, u32[]{:S(2)}, u32[]{:S(2)}) collective-permute-start(f32[1,27,16,128]{3,2,1,0:T(8,128)} %slice.322), channel_id=1, source_target_pairs={{2,0},{4,2},{6,4},{8,6},{10,8},{12,10},{14,12},{16,14},{18,16},{20... | collective-permute-start | bytes 663560 | tf_op jit(solution)/shard_map/ppermute | solution.py:15
  18.7 4.6 copy-start.27
  20.1 6.4 collective-permute-start.1
  23.3 3.2 copy-start.24
  23.3 3.2 copy-start.26
  23.3 3.2 copy-start.28
  241.2 4.9 copy-start.5
  241.2 4.9 copy-start.6
  241.2 4.9 copy-start.7
  241.2 4.9 copy-start.9
  241.2 4.9 copy-start.11
  241.2 4.9 copy-start.13
  241.2 4.9 copy-start.15
  241.2 4.9 copy-start.17
  241.2 4.9 copy-start.19
  241.4 24.0 %collective-permute-start.2 = (f32[8,27,16,128]{3,0,2,1:T(8,128)S(1)}, f32[8,27,16,128]{3,0,2,1:T(8,128)S(1)}, u32[]{:S(2)}, u32[]{:S(2)}) collective-permute-start(f32[8,27,16,128]{3,0,2,1:T(8,128)S(1)} %slice.428), channel_id=1, source_target_pairs={{2,0},{4,2},{6,4},{8,6},{10,8},{12,10},{14,12},{16,14},{18,16},{20... | collective-permute-start | bytes 5308424 | tf_op jit(solution)/shard_map/ppermute | solution.py:15
  252.6 21.4 %collective-permute-start.3 = (f32[8,27,16,128]{3,0,2,1:T(8,128)S(1)}, f32[8,27,16,128]{3,0,2,1:T(8,128)S(1)}, u32[]{:S(2)}, u32[]{:S(2)}) collective-permute-start(f32[8,27,16,128]{3,0,2,1:T(8,128)S(1)} %fusion.76), channel_id=1, source_target_pairs={{0,2},{2,4},{4,6},{6,8},{8,10},{10,12},{12,14},{14,16},{16,18},{18... | collective-permute-start | bytes 5308424 | tf_op jit(solution)/shard_map/ppermute | solution.py:15
  265.3 8.6 %copy-start.31 = (f32[8,27,16,128]{3,0,2,1:T(8,128)}, f32[8,27,16,128]{3,0,2,1:T(8,128)S(1)}, u32[]{:S(2)}) copy-start(f32[8,27,16,128]{3,0,2,1:T(8,128)S(1)} %collective-permute-done.2) | copy-start | bytes 5308420
  294.7 24.6 %collective-permute-start.4 = (f32[8,27,16,128]{3,0,2,1:T(8,128)S(1)}, f32[8,27,16,128]{3,0,2,1:T(8,128)S(1)}, u32[]{:S(2)}, u32[]{:S(2)}) collective-permute-start(f32[8,27,16,128]{3,0,2,1:T(8,128)S(1)} %slice.436), channel_id=1, source_target_pairs={{2,0},{4,2},{6,4},{8,6},{10,8},{12,10},{14,12},{16,14},{18,16},{20... | collective-permute-start | bytes 5308424 | tf_op jit(solution)/shard_map/ppermute | solution.py:15
  296.6 25.4 %copy-start.4 = (f32[8,32,16,128]{3,0,2,1:T(8,128)S(1)}, f32[8,32,16,128]{3,0,2,1:T(8,128)}, u32[]{:S(2)}) copy-start(f32[8,32,16,128]{3,0,2,1:T(8,128)} %get-tuple-element.8) | copy-start | bytes 6291460
  296.8 24.0 %collective-permute-start.5 = (f32[8,27,16,128]{3,0,2,1:T(8,128)S(1)}, f32[8,27,16,128]{3,0,2,1:T(8,128)S(1)}, u32[]{:S(2)}, u32[]{:S(2)}) collective-permute-start(f32[8,27,16,128]{3,0,2,1:T(8,128)S(1)} %fusion.79), channel_id=1, source_target_pairs={{0,2},{2,4},{4,6},{6,8},{8,10},{10,12},{12,14},{14,16},{16,18},{18... | collective-permute-start | bytes 5308424 | tf_op jit(solution)/shard_map/ppermute | solution.py:15
  548.6 7.1 copy-start.34
  (19 other events, 28.7 us)
Sparse Core Ops, SparseCore 0:
  11.6 66.3 all-gather.2
  333.4 65.5 all-gather.4
where the time goes:
time: 727 us
  blocking collectives  426 us (59%)
  waiting for transfers between devices  155 us (21%)
  other arithmetic  54.6 us (8%)
  matrix products  41.2 us (6%)
  starting transfers between devices  19.7 us (3%)
  local copies, waits for them, and re-layouts  15.7 us (2%)
  between operations  14.6 us (2%)
    psum x3, blocking collectives, total_one(): summed = lax.psum(partial_sum, 'brick')  426 us
    all_gather x2, waiting for transfers between devices, to_work(): work_rows = lax.all_gather(flat_block, 'vec', axis=0, tiled=True)  115 us
    ppermute x6, waiting for transfers between devices, passed_along(): return lax.ppermute(value, axis, pairs)  40.2 us
    mul x4, other arithmetic, local_planes(): channel * field_in  25.2 us
    dot_general x3, matrix products, inner_of(): return jnp.einsum('in,jn->ij', left_rows, right_rows, precision=highest)  23.3 us
    ppermute x6, starting transfers between devices, passed_along(): return lax.ppermute(value, axis, pairs)  19.7 us
  transfers between devices with their start and end apart: 8, of which 7 were waited for; matrix products, arithmetic and copies ran while one was open for 2% of the time, Pallas kernels for 0%

commit v1 on v0

--- a/solution.py
+++ b/solution.py
@@ -93,7 +93,7 @@
         return own_rows.reshape(grid_shape)
 
     def total_one(partial_sum):
-        summed = lax.psum(partial_sum, "brick")
+        summed = jnp.sum(lax.all_gather(partial_sum, "brick"), axis=0)
         return summed
 
     start_work = to_work(start_block.astype(jnp.float32))

time: 727 us -> 539 us (0.74)
  blocking collectives: 426 us -> 242 us
    psum x3 -> x0, blocking collectives: 426 us -> none  [total_one(): summed = lax.psum(partial_sum, 'brick')]
    all_gather x0 -> x3, blocking collectives: none -> 242 us  [total_one(): summed = jnp.sum(lax.all_gather(partial_sum, 'brick'), axis=0)]
  transfers between devices with their start and end apart: 8 -> 8, of which waited for: 7 -> 7; matrix products, arithmetic and copies ran while one was open for 2% -> 3% of each run, Pallas kernels for 0% -> 0%
where the time goes in v1:
time: 539 us; the launch traced here: 538 us
  blocking collectives  242 us (45%)
  waiting for transfers between devices  154 us (29%)
  other arithmetic  54.8 us (10%)
  matrix products  41.1 us (8%)
  starting transfers between devices  18.9 us (4%)
  between operations  14.5 us (3%)
  local copies, waits for them, and re-layouts  13.8 us (3%)
    all_gather x3, blocking collectives, total_one(): summed = jnp.sum(lax.all_gather(partial_sum, 'brick'), axis=0)  242 us
    all_gather x2, waiting for transfers between devices, to_work(): work_rows = lax.all_gather(flat_block, 'vec', axis=0, tiled=True)  113 us
    ppermute x6, waiting for transfers between devices, passed_along(): return lax.ppermute(value, axis, pairs)  40.4 us
    mul x4, other arithmetic, local_planes(): channel * field_in  25.2 us
    dot_general x3, matrix products, inner_of(): return jnp.einsum('in,jn->ij', left_rows, right_rows, precision=highest)  23.2 us
    ppermute x6, starting transfers between devices, passed_along(): return lax.ppermute(value, axis, pairs)  18.8 us
    mul x2, other arithmetic, half_step(): return 0.5 * (block_in + inv_root * affinity_apply(inv_root * block_in))  13.9 us
    unnamed x72, local copies, waits for them, and re-layouts  11.7 us
  transfers between devices with their start and end apart: 8, of which 7 were waited for; matrix products, arithmetic and copies ran while one was open for 3% of the time, Pallas kernels for 0%

profile of v1, /device:TPU:1, one launch (start us, length us, event | category | flops | bytes accessed | tf_op | source)
XLA Modules:
  0.0 538.4 jit_solution(2198922283831312319)
XLA Ops:
  9.0 2.5 copy.13
  12.3 3.3 collective-permute-start
  20.1 3.2 collective-permute-start.1
  26.5 2.7 broadcast_multiply_fusion.24
  29.2 48.8 %all-gather.6.cloned.1.call-done = f32[16,65536]{1,0:T(8,128)} async-done(((f32[8,65536]{1,0:T(8,128)}), f32[16,65536]{1,0:T(8,128)}) %all-gather.6.cloned.1.call-update) | async-done | bytes 4194320 | tf_op jit(solution)/shard_map/all_gather | solution.py:86
  78.0 8.6 %fusion.127 = f32[16,16]{1,0:T(8,128)S(1)} fusion(f32[16,65536]{1,0:T(8,128)} %all-gather.6.cloned.1.call-done), kind=kOutput, calls=%fused_computation.264 | convolution fusion | flops 201326592 | bytes 4195328 | tf_op jit(solution)/shard_map/in,jn->ij/dot_general | solution.py:64
  86.6 80.8 %all-gather = f32[1024,16]{1,0:T(8,128)S(1)} all-gather(f32[16,16]{1,0:T(8,128)S(1)} %fusion.127), channel_id=2, replica_groups=mesh['brick'=64,'vec'=2] {'brick'}, dimensions={0}, use_global_device_ids=true | all-gather | bytes 66560 | tf_op jit(solution)/shard_map/all_gather | solution.py:96
  171.5 5.4 %fusion.122 = f32[16,65536]{1,0:T(8,128)S(1)} fusion(f32[16,65536]{1,0:T(8,128)} %all-gather.6.cloned.1.call-done, f32[1,16,16]{1,2,0:T(8,128)S(1)} %custom-call.6), kind=kOutput, calls=%fused_computation.238 | convolution fusion | flops 201326592 | bytes 8389632 | tf_op jit(solution)/shard_map/triangular_solve/dot.1 | solution.py:101
  183.6 5.1 broadcast_multiply_fusion.12
  190.1 3.5 collective-permute-start.3
  193.6 11.5 %collective-permute-done.2 = f32[8,27,16,128]{3,0,2,1:T(8,128)S(1)} collective-permute-done((f32[8,27,16,128]{3,0,2,1:T(8,128)S(1)}, f32[8,27,16,128]{3,0,2,1:T(8,128)S(1)}, u32[]{:S(2)}, u32[]{:S(2)}) %collective-permute-start.2) | collective-permute-done | bytes 1769504 | tf_op jit(solution)/shard_map/ppermute | solution.py:15
  205.1 7.9 %collective-permute-done.3 = f32[8,27,16,128]{3,0,2,1:T(8,128)S(1)} collective-permute-done((f32[8,27,16,128]{3,0,2,1:T(8,128)S(1)}, f32[8,27,16,128]{3,0,2,1:T(8,128)S(1)}, u32[]{:S(2)}, u32[]{:S(2)}) %collective-permute-start.3) | collective-permute-done | bytes 1769504 | tf_op jit(solution)/shard_map/ppermute | solution.py:15
  214.3 12.9 %broadcast_multiply_fusion.13 = (f32[8,32,16,128]{3,0,2,1:T(8,128)}, f32[8,32,16,128]{3,0,2,1:T(8,128)S(1)}, f32[8,32,16,128]{3,0,2,1:T(8,128)}) fusion(f32[32,16,128]{2,1,0:T(8,128)} %get-tuple-element.23, f32[32,16,128]{2,1,0:T(8,128)} %get-tuple-element.14, f32[8,32,16,128]{3,0,2,1:T(8,128)} %bitcast.70, f32[8,27,16,128]{3,0,2,1:T(8,128)} %copy-done.32, ...), kind=kLoop, calls=%fused_computation.155 | loop fusion | flops 22020096 | bytes 40763392 | tf_op jit(solution)/shard_map/mul | solution.py:39
  228.7 5.1 broadcast_multiply_fusion.11
  235.9 4.5 collective-permute-start.5
  240.4 17.9 %collective-permute-done.4 = f32[8,27,16,128]{3,0,2,1:T(8,128)S(1)} collective-permute-done((f32[8,27,16,128]{3,0,2,1:T(8,128)S(1)}, f32[8,27,16,128]{3,0,2,1:T(8,128)S(1)}, u32[]{:S(2)}, u32[]{:S(2)}) %collective-permute-start.4) | collective-permute-done | bytes 1769504 | tf_op jit(solution)/shard_map/ppermute | solution.py:15
  261.1 11.3 %add_multiply_fusion.1 = f32[8,32,16,128]{3,0,2,1:T(8,128)} fusion(f32[8,32,16,128]{3,0,2,1:T(8,128)} %get-tuple-element.13, f32[8,27,16,128]{3,0,2,1:T(8,128)} %copy-done.30, f32[8,32,16,128]{3,0,2,1:T(8,128)} %get-tuple-element.43, f32[8,32,16,128]{3,0,2,1:T(8,128)S(1)} %get-tuple-element.12, f32[8,32,16,128]{3,0,2,1:T(8,128)} %get-tuple-element.50, ...), kind=kLoop, calls=%fused_computation.134 | loop fusion | flops 22020096 | bytes 36306944 | tf_op jit(solution)/shard_map/mul | solution.py:78
  272.4 64.3 %all-gather.8.cloned.1.call-done = f32[16,65536]{1,0:T(8,128)} async-done(((f32[8,65536]{1,0:T(8,128)}), f32[16,65536]{1,0:T(8,128)}) %all-gather.8.cloned.1.call-update) | async-done | bytes 4194320 | tf_op jit(solution)/shard_map/all_gather | solution.py:86
  336.7 8.8 %fusion.128 = f32[16,16]{1,0:T(8,128)S(1)} fusion(f32[16,65536]{1,0:T(8,128)} %all-gather.8.cloned.1.call-done, f32[16,65536]{1,0:T(8,128)} %copy-done.1), kind=kOutput, calls=%fused_computation.265 | convolution fusion | flops 201326592 | bytes 8389632 | tf_op jit(solution)/shard_map/in,jn->ij/dot_general | solution.py:64
  345.6 83.1 %all-gather.1 = f32[1024,16]{1,0:T(8,128)S(1)} all-gather(f32[16,16]{1,0:T(8,128)S(1)} %fusion.128), channel_id=3, replica_groups=mesh['brick'=64,'vec'=2] {'brick'}, dimensions={0}, use_global_device_ids=true | all-gather | bytes 66560 | tf_op jit(solution)/shard_map/all_gather | solution.py:96
  428.7 7.1 %convolution_subtract_fusion = f32[16,65536]{1,0:T(8,128)S(1)} fusion(f32[16,65536]{1,0:T(8,128)} %all-gather.8.cloned.1.call-done, f32[16,16]{1,0:T(8,128)S(1)} %reduce_sum.28, f32[16,65536]{1,0:T(8,128)} %copy-done.1), kind=kOutput, calls=%fused_computation | convolution fusion | flops 202375168 | bytes 12583936 | tf_op jit(solution)/shard_map/ij,jn->in/dot_general | solution.py:105
  435.9 5.8 %fusion.129 = f32[16,16]{1,0:T(8,128)S(1)} fusion(f32[16,65536]{1,0:T(8,128)S(1)} %convolution_subtract_fusion), kind=kOutput, calls=%fused_computation.266 | convolution fusion | flops 201326592 | bytes 4195328 | tf_op jit(solution)/shard_map/in,jn->ij/dot_general | solution.py:64
  441.6 77.9 %all-gather.2 = f32[1024,16]{1,0:T(8,128)S(1)} all-gather(f32[16,16]{1,0:T(8,128)S(1)} %fusion.129), channel_id=4, replica_groups=mesh['brick'=64,'vec'=2] {'brick'}, dimensions={0}, use_global_device_ids=true | all-gather | bytes 66560 | tf_op jit(solution)/shard_map/all_gather | solution.py:96
  524.3 5.4 %fusion.119 = f32[16,65536]{1,0:T(8,128)S(1)} fusion(f32[16,65536]{1,0:T(8,128)} %copy-done, f32[1,16,16]{1,2,0:T(8,128)S(1)} %custom-call.7), kind=kOutput, calls=%fused_computation.234 | convolution fusion | flops 201326592 | bytes 8389632 | tf_op jit(solution)/shard_map/triangular_solve/dot.1 | solution.py:108
  (111 shorter events, 36.4 us)
Async XLA Ops:
  7.2 70.8 %all-gather.6.cloned.1.call-start = ((), (), s32[]{:S(2)}) async-start(), calls=%async_computation | async-start | bytes 6291456 | tf_op jit(solution)/shard_map/all_gather | solution.py:86
  11.5 325.2 %all-gather.8.cloned.1.call-start = ((), (), s32[]{:S(2)}) async-start(), calls=%async_computation.1 | async-start | bytes 6291456 | tf_op jit(solution)/shard_map/all_gather | solution.py:86
  12.3 12.7 %collective-permute-start = (f32[1,27,16,128]{3,2,1,0:T(8,128)}, f32[1,27,16,128]{3,2,1,0:T(8,128)}, u32[]{:S(2)}, u32[]{:S(2)}) collective-permute-start(f32[1,27,16,128]{3,2,1,0:T(8,128)} %slice.322), channel_id=1, source_target_pairs={{2,0},{4,2},{6,4},{8,6},{10,8},{12,10},{14,12},{16,14},{18,16},{20... | collective-permute-start | bytes 663560 | tf_op jit(solution)/shard_map/ppermute | solution.py:15
  18.7 4.6 copy-start.27
  20.1 6.4 %collective-permute-start.1 = (f32[1,27,16,128]{3,2,1,0:T(8,128)}, f32[1,27,16,128]{3,2,1,0:T(8,128)}, u32[]{:S(2)}, u32[]{:S(2)}) collective-permute-start(f32[1,27,16,128]{3,2,1,0:T(8,128)} %fusion.117), channel_id=1, source_target_pairs={{0,2},{2,4},{4,6},{6,8},{8,10},{10,12},{12,14},{14,16},{16,18},{18... | collective-permute-start | bytes 663560 | tf_op jit(solution)/shard_map/ppermute | solution.py:15
  23.3 3.2 copy-start.24
  23.3 3.2 copy-start.26
  23.3 3.2 copy-start.28
  23.3 3.2 copy-start.33
  181.0 2.6 copy-start.7
  181.0 2.6 copy-start.9
  181.0 2.6 copy-start.11
  181.0 2.6 copy-start.13
  181.0 2.6 copy-start.15
  181.0 2.6 copy-start.17
  181.0 2.6 copy-start.19
  181.2 24.0 %collective-permute-start.2 = (f32[8,27,16,128]{3,0,2,1:T(8,128)S(1)}, f32[8,27,16,128]{3,0,2,1:T(8,128)S(1)}, u32[]{:S(2)}, u32[]{:S(2)}) collective-permute-start(f32[8,27,16,128]{3,0,2,1:T(8,128)S(1)} %slice.428), channel_id=1, source_target_pairs={{2,0},{4,2},{6,4},{8,6},{10,8},{12,10},{14,12},{16,14},{18,16},{20... | collective-permute-start | bytes 5308424 | tf_op jit(solution)/shard_map/ppermute | solution.py:15
  190.1 22.9 %collective-permute-start.3 = (f32[8,27,16,128]{3,0,2,1:T(8,128)S(1)}, f32[8,27,16,128]{3,0,2,1:T(8,128)S(1)}, u32[]{:S(2)}, u32[]{:S(2)}) collective-permute-start(f32[8,27,16,128]{3,0,2,1:T(8,128)S(1)} %fusion.76), channel_id=1, source_target_pairs={{0,2},{2,4},{4,6},{6,8},{8,10},{10,12},{12,14},{14,16},{16,18},{18... | collective-permute-start | bytes 5308424 | tf_op jit(solution)/shard_map/ppermute | solution.py:15
  205.1 7.9 %copy-start.31 = (f32[8,27,16,128]{3,0,2,1:T(8,128)}, f32[8,27,16,128]{3,0,2,1:T(8,128)S(1)}, u32[]{:S(2)}) copy-start(f32[8,27,16,128]{3,0,2,1:T(8,128)S(1)} %collective-permute-done.2) | copy-start | bytes 5308420
  233.8 24.6 %collective-permute-start.4 = (f32[8,27,16,128]{3,0,2,1:T(8,128)S(1)}, f32[8,27,16,128]{3,0,2,1:T(8,128)S(1)}, u32[]{:S(2)}, u32[]{:S(2)}) collective-permute-start(f32[8,27,16,128]{3,0,2,1:T(8,128)S(1)} %slice.436), channel_id=1, source_target_pairs={{2,0},{4,2},{6,4},{8,6},{10,8},{12,10},{14,12},{16,14},{18,16},{20... | collective-permute-start | bytes 5308424 | tf_op jit(solution)/shard_map/ppermute | solution.py:15
  235.7 25.4 %copy-start.4 = (f32[8,32,16,128]{3,0,2,1:T(8,128)S(1)}, f32[8,32,16,128]{3,0,2,1:T(8,128)}, u32[]{:S(2)}) copy-start(f32[8,32,16,128]{3,0,2,1:T(8,128)} %get-tuple-element.11) | copy-start | bytes 6291460
  235.9 24.0 %collective-permute-start.5 = (f32[8,27,16,128]{3,0,2,1:T(8,128)S(1)}, f32[8,27,16,128]{3,0,2,1:T(8,128)S(1)}, u32[]{:S(2)}, u32[]{:S(2)}) collective-permute-start(f32[8,27,16,128]{3,0,2,1:T(8,128)S(1)} %fusion.79), channel_id=1, source_target_pairs={{0,2},{2,4},{4,6},{6,8},{8,10},{10,12},{12,14},{14,16},{16,18},{18... | collective-permute-start | bytes 5308424 | tf_op jit(solution)/shard_map/ppermute | solution.py:15
  428.7 7.1 %copy-start.34 = (f32[16,16]{1,0:T(8,128)}, f32[16,16]{1,0:T(8,128)S(1)}, u32[]{:S(2)}) copy-start(f32[16,16]{1,0:T(8,128)S(1)} %reduce_sum.28) | copy-start | bytes 3076
  435.9 5.8 %copy-start = (f32[16,65536]{1,0:T(8,128)}, f32[16,65536]{1,0:T(8,128)S(1)}, u32[]{:S(2)}) copy-start(f32[16,65536]{1,0:T(8,128)S(1)} %convolution_subtract_fusion) | copy-start | bytes 12582916
  (19 other events, 28.7 us)
Sparse Core Ops, SparseCore 0:
  11.6 66.3 all-gather.5
  272.5 64.1 all-gather.7
